TPU v7x, 32 devices: a whole 2x2x4 slice. The times are simulated.
32 devices in a mesh: grp: 2 (over x), tm: 16 (over z, y, core).
Axes of the slice: x: 2, y: 2, z: 4, core: 2. Of those that a mesh axis runs over, the one named last changes fastest.
Arguments:
- upsampled: bfloat16 [2, 12288, 512], P(None, ('grp', 'tm')), parts along dimension 1, may hold values from -6 to 6
- taps: bfloat16 [3, 7, 512, 512], replicated, may hold values from -0.09375 to 0.09375
- bias_wide: float32 [3, 512], replicated, may hold values from -1.8 to 1.8
- pointwise: bfloat16 [3, 512, 512], replicated, may hold values from -0.25 to 0.25
- bias_point: float32 [3, 512], replicated, may hold values from -1.8 to 1.8
- alpha_in: float32 [3, 512], replicated, may hold values from 0.5 to 4
- beta_in: float32 [3, 512], replicated, may hold values from 0.5 to 4
- alpha_mid: float32 [3, 512], replicated, may hold values from 0.5 to 4
- beta_mid: float32 [3, 512], replicated, may hold values from 0.5 to 4
Outputs:
- decoded: bfloat16 [12288, 512], P(('grp', 'tm')), parts along dimension 0
There are 2 independent parts, one for each index of `grp`. A program takes and returns all parts, laid end to end along the dimension named above; an argument that names none is the same for every part. Nothing has to cross between parts.
All inputs are finite; a program needn't handle non-finite values.
Results may differ from a plain program's by a relative error of at most 0.027.
The roundings to bfloat16 on the way count: a program that leaves them out, or rounds other values in their place, can miss the bound.
Values may be sent and summed in bfloat16 or wider, within the bound.
A program may use at most 128 MiB of HBM per device.

v0:
```python
import jax
import jax.numpy as jnp
from jax import lax
from jax.sharding import PartitionSpec as P

KERNEL = 7
STRIDE = 8
UNITS = 3


def passed_along(value, axis, steps):
    count = lax.axis_size(axis)
    first, last = (max(0, -steps), min(count, count - steps))
    return lax.ppermute(value, axis, [(source, source + steps) for source in range(first, last)])


def with_halo(block, sides, width):
    for axis, dim in sides:
        count = lax.axis_size(axis)
        forward = [(i, i + 1) for i in range(count - 1)]
        backward = [(target, source) for source, target in forward]
        low = lax.ppermute(
            lax.slice_in_dim(block, block.shape[dim] - width, None, axis=dim), axis, forward
        )
        high = lax.ppermute(lax.slice_in_dim(block, 0, width, axis=dim), axis, backward)
        block = jnp.concatenate([low, block, high], axis=dim)
    return block


def snake(values, alpha, beta):
    return values + jnp.square(jnp.sin(alpha * values)) / beta


def residual_unit(
    inputs, dilation, taps, bias_wide, pointwise, bias_point, alpha_in, beta_in, alpha_mid, beta_mid
):
    length = inputs.shape[0] - 6 * dilation
    widened = snake(inputs.astype(jnp.float32), alpha_in, beta_in).astype(jnp.bfloat16)
    stacked = jnp.concatenate(
        [widened[k * dilation : k * dilation + length] for k in range(KERNEL)], axis=1
    )
    kernel = taps.reshape(KERNEL * taps.shape[1], taps.shape[2])
    middle = jnp.dot(stacked, kernel, preferred_element_type=jnp.float32) + bias_wide
    gated = snake(middle, alpha_mid, beta_mid).astype(jnp.bfloat16)
    update = jnp.dot(gated, pointwise, preferred_element_type=jnp.float32) + bias_point
    kept = inputs[3 * dilation : 3 * dilation + length].astype(jnp.float32)
    return (kept + update).astype(jnp.bfloat16)


def per_device(
    upsampled, taps, bias_wide, pointwise, bias_point, alpha_in, beta_in, alpha_mid, beta_mid
):
    frames = upsampled.shape[1]
    dilations = (1, 3, 9)
    carried = passed_along(upsampled[1, frames - STRIDE :], "tm", 1)
    later = jnp.concatenate([carried, upsampled[1, : frames - STRIDE]], axis=0)
    current = (upsampled[0].astype(jnp.float32) + later.astype(jnp.float32)).astype(jnp.bfloat16)
    for index in range(UNITS):
        padded = with_halo(current, (("tm", 0),), 3 * dilations[index])
        current = residual_unit(
            padded,
            dilations[index],
            taps[index],
            bias_wide[index],
            pointwise[index],
            bias_point[index],
            alpha_in[index],
            beta_in[index],
            alpha_mid[index],
            beta_mid[index],
        )
    return current


def solution(mesh):
    placed = (P(None, ("grp", "tm"), None), P(), P(), P(), P(), P(), P(), P(), P())
    return jax.shard_map(
        per_device, mesh=mesh, in_specs=placed, out_specs=P(("grp", "tm"), None), check_vma=False
    )
```

profile of v0, /device:TPU:5, one launch (start us, length us, event | category | flops | bytes accessed | tf_op | source)
XLA Modules:
  0.0 73.5 jit_solution(8115087615131059547)
XLA Ops:
  0.0 0.7 slice_bitcast_fusion.1
  0.7 3.7 %collective-permute-start = (bf16[8,512]{1,0:T(8,128)(2,1)S(1)}, bf16[8,512]{1,0:T(8,128)(2,1)S(1)}, u32[]{:S(2)}, u32[]{:S(2)}) collective-permute-start(bf16[8,512]{1,0:T(8,128)(2,1)S(1)} %slice_bitcast_fusion.1), channel_id=1, source_target_pairs={{0,1},{1,2},{2,3},{3,4},{4,5},{5,6},{6,7},{7,8},{8,9},{9,10},{10,1... | collective-permute-start | bytes 24584 | tf_op jit(solution)/shard_map/ppermute | solution.py:14
  4.4 1.0 %slice_bitcast_fusion = bf16[376,512]{1,0:T(8,128)(2,1)S(1)} fusion(bf16[2,384,512]{2,1,0:T(8,128)(2,1)} %param.9), kind=kLoop, calls=%fused_computation.71 | loop fusion | bytes 770048 | tf_op jit(solution)/shard_map/squeeze | solution.py:56
  5.4 1.4 %fusion.38 = (f32[1,512]{1,0:T(1,128)}, f32[1,512]{1,0:T(1,128)}, f32[1,512]{1,0:T(1,128)}) fusion(f32[3,512]{1,0:T(4,128)} %param.11), kind=kLoop, calls=%fused_computation.77 | loop fusion | bytes 12288 | tf_op jit(solution)/shard_map/slice | solution.py:64
  6.8 1.4 %fusion.41 = (f32[1,512]{1,0:T(1,128)}, f32[1,512]{1,0:T(1,128)}, f32[1,512]{1,0:T(1,128)}) fusion(f32[3,512]{1,0:T(4,128)} %param.13), kind=kLoop, calls=%fused_computation.80 | loop fusion | bytes 12288 | tf_op jit(solution)/shard_map/slice | solution.py:66
  8.2 0.8 %fusion.42 = (f32[1,512]{1,0:T(1,128)S(1)}, f32[1,512]{1,0:T(1,128)S(1)}, f32[1,512]{1,0:T(1,128)S(1)}) fusion(f32[3,512]{1,0:T(4,128)} %param.14), kind=kLoop, calls=%fused_computation.81 | loop fusion | bytes 12288 | tf_op jit(solution)/shard_map/slice | solution.py:67
  9.1 0.8 %fusion.43 = (f32[1,512]{1,0:T(1,128)S(1)}, f32[1,512]{1,0:T(1,128)S(1)}, f32[1,512]{1,0:T(1,128)S(1)}) fusion(f32[3,512]{1,0:T(4,128)} %param.15), kind=kLoop, calls=%fused_computation.82 | loop fusion | bytes 12288 | tf_op jit(solution)/shard_map/slice | solution.py:68
  9.9 0.0 copy-start
  9.9 0.0 copy-start.2
  9.9 7.4 %fusion.34 = (bf16[1,7,512,512]{3,2,1,0:T(8,128)(2,1)}, bf16[1,7,512,512]{3,2,1,0:T(8,128)(2,1)}, bf16[1,7,512,512]{3,2,1,0:T(8,128)(2,1)}) fusion(bf16[3,7,512,512]{3,2,1,0:T(8,128)(2,1)} %param.10), kind=kLoop, calls=%fused_computation.73 | loop fusion | bytes 22020096 | tf_op jit(solution)/shard_map/slice | solution.py:63
  17.3 0.6 fusion.39
  17.9 0.1 fusion.18
  18.0 1.9 %collective-permute-start.1 = (bf16[3,512]{1,0:T(4,128)(2,1)S(1)}, bf16[3,512]{1,0:T(4,128)(2,1)S(1)}, u32[]{:S(2)}, u32[]{:S(2)}) collective-permute-start(bf16[3,512]{1,0:T(4,128)(2,1)S(1)} %get-tuple-element.12), channel_id=1, source_target_pairs={{0,1},{1,2},{2,3},{3,4},{4,5},{5,6},{6,7},{7,8},{8,9},{9,10},{10,1... | collective-permute-start | bytes 9224 | tf_op jit(solution)/shard_map/ppermute | solution.py:22
  20.0 2.4 %collective-permute-start.2 = (bf16[3,512]{1,0:T(4,128)(2,1)S(1)}, bf16[3,512]{1,0:T(4,128)(2,1)S(1)}, u32[]{:S(2)}, u32[]{:S(2)}) collective-permute-start(bf16[3,512]{1,0:T(4,128)(2,1)S(1)} %get-tuple-element.13), channel_id=1, source_target_pairs={{1,0},{2,1},{3,2},{4,3},{5,4},{6,5},{7,6},{8,7},{9,8},{10,9},{11,1... | collective-permute-start | bytes 9224 | tf_op jit(solution)/shard_map/ppermute | solution.py:25
  22.4 0.6 fusion.40
  23.0 2.8 %collective-permute-done.2 = bf16[3,512]{1,0:T(4,128)(2,1)S(1)} collective-permute-done((bf16[3,512]{1,0:T(4,128)(2,1)S(1)}, bf16[3,512]{1,0:T(4,128)(2,1)S(1)}, u32[]{:S(2)}, u32[]{:S(2)}) %collective-permute-start.2) | collective-permute-done | bytes 3104 | tf_op jit(solution)/shard_map/ppermute | solution.py:25
  25.8 2.8 %fusion.17 = bf16[390,512]{1,0:T(8,128)(2,1)S(1)} fusion(bf16[3,512]{1,0:T(4,128)(2,1)S(1)} %collective-permute-done.2, bf16[384,512]{1,0:T(8,128)(2,1)S(1)} %fusion.18, bf16[3,512]{1,0:T(4,128)(2,1)S(1)} %collective-permute-done.1, f32[512]{0:T(512)S(1)} %bitcast.51, f32[512]{0:T(512)S(1)} %bitcast.50), kind=kLoop, calls=%fused_computation.29 | loop fusion | flops 2196480 | bytes 802816 | tf_op jit(solution)/shard_map/convert_element_type | solution.py:38
  28.7 0.1 slice_dynamic-update-slice_fusion.19
  28.8 0.1 slice_dynamic-update-slice_fusion.18
  28.9 0.1 slice_dynamic-update-slice_fusion.17
  29.0 0.1 slice_dynamic-update-slice_fusion.16
  29.1 0.1 slice_dynamic-update-slice_fusion.15
  29.2 0.1 slice_dynamic-update-slice_fusion.14
  29.3 6.5 %fusion.5 = bf16[384,512]{1,0:T(8,128)(2,1)S(1)} fusion(bf16[384,3584]{1,0:T(8,128)(2,1)S(1)} %slice_dynamic-update-slice_fusion.14, bf16[3584,512]{1,0:T(8,128)(2,1)} %bitcast.45, bf16[384,512]{1,0:T(8,128)(2,1)S(1)} %fusion.18, bf16[3,512,512]{2,1,0:T(8,128)(2,1)} %param.12, f32[512]{0:T(512)} %bitcast.61, f32[512]{0:T(512)} %bitcast.63, ...), kind=kOutput, calls=%fused_computation.11 | convolution fusion | flops 1612578816 | bytes 7741440 | tf_op jit(solution)/shard_map/dot_general | solution.py:45
  35.8 1.9 %collective-permute-start.3 = (bf16[9,512]{1,0:T(8,128)(2,1)S(1)}, bf16[9,512]{1,0:T(8,128)(2,1)S(1)}, u32[]{:S(2)}, u32[]{:S(2)}) collective-permute-start(bf16[9,512]{1,0:T(8,128)(2,1)S(1)} %get-tuple-element.10), channel_id=1, source_target_pairs={{0,1},{1,2},{2,3},{3,4},{4,5},{5,6},{6,7},{7,8},{8,9},{9,10},{10,1... | collective-permute-start | bytes 27656 | tf_op jit(solution)/shard_map/ppermute | solution.py:22
  37.7 2.6 %collective-permute-start.4 = (bf16[9,512]{1,0:T(8,128)(2,1)S(1)}, bf16[9,512]{1,0:T(8,128)(2,1)S(1)}, u32[]{:S(2)}, u32[]{:S(2)}) collective-permute-start(bf16[9,512]{1,0:T(8,128)(2,1)S(1)} %get-tuple-element.11), channel_id=1, source_target_pairs={{1,0},{2,1},{3,2},{4,3},{5,4},{6,5},{7,6},{8,7},{9,8},{10,9},{11,1... | collective-permute-start | bytes 27656 | tf_op jit(solution)/shard_map/ppermute | solution.py:25
  40.3 3.4 %collective-permute-done.4 = bf16[9,512]{1,0:T(8,128)(2,1)S(1)} collective-permute-done((bf16[9,512]{1,0:T(8,128)(2,1)S(1)}, bf16[9,512]{1,0:T(8,128)(2,1)S(1)}, u32[]{:S(2)}, u32[]{:S(2)}) %collective-permute-start.4) | collective-permute-done | bytes 9248 | tf_op jit(solution)/shard_map/ppermute | solution.py:25
  43.7 3.4 %fusion.13 = bf16[402,512]{1,0:T(8,128)(2,1)S(1)} fusion(bf16[9,512]{1,0:T(8,128)(2,1)S(1)} %collective-permute-done.4, bf16[384,512]{1,0:T(8,128)(2,1)S(1)} %fusion.5, bf16[9,512]{1,0:T(8,128)(2,1)S(1)} %collective-permute-done.3, f32[512]{0:T(512)S(1)} %bitcast.49, f32[512]{0:T(512)S(1)} %bitcast.48), kind=kLoop, calls=%fused_computation.25 | loop fusion | flops 2264064 | bytes 827392 | tf_op jit(solution)/shard_map/convert_element_type | solution.py:38
  47.2 0.1 slice_dynamic-update-slice_fusion.12
  47.3 0.1 slice_dynamic-update-slice_fusion.11
  47.4 0.1 slice_dynamic-update-slice_fusion.10
  47.5 0.1 slice_dynamic-update-slice_fusion.9
  47.6 0.1 slice_dynamic-update-slice_fusion.8
  47.7 0.1 slice_dynamic-update-slice_fusion.7
  47.8 0.0 copy-done.7
  47.8 0.0 copy-done.8
  47.8 6.5 %fusion.4 = bf16[384,512]{1,0:T(8,128)(2,1)S(1)} fusion(bf16[384,3584]{1,0:T(8,128)(2,1)S(1)} %slice_dynamic-update-slice_fusion.7, bf16[3584,512]{1,0:T(8,128)(2,1)} %bitcast.44, bf16[384,512]{1,0:T(8,128)(2,1)S(1)} %fusion.5, bf16[3,512,512]{2,1,0:T(8,128)(2,1)} %param.12, f32[512]{0:T(512)S(1)} %bitcast.57, f32[512]{0:T(512)} %bitcast.59, ...), kind=kOutput, calls=%fused_computation.10 | convolution fusion | flops 1612578816 | bytes 7741440 | tf_op jit(solution)/shard_map/dot_general | solution.py:45
  54.3 1.9 %collective-permute-start.5 = (bf16[27,512]{1,0:T(8,128)(2,1)S(1)}, bf16[27,512]{1,0:T(8,128)(2,1)S(1)}, u32[]{:S(2)}, u32[]{:S(2)}) collective-permute-start(bf16[27,512]{1,0:T(8,128)(2,1)S(1)} %get-tuple-element.8), channel_id=1, source_target_pairs={{0,1},{1,2},{2,3},{3,4},{4,5},{5,6},{6,7},{7,8},{8,9},{9,10},{10,1... | collective-permute-start | bytes 82952 | tf_op jit(solution)/shard_map/ppermute | solution.py:22
  56.3 2.4 %collective-permute-start.6 = (bf16[27,512]{1,0:T(8,128)(2,1)S(1)}, bf16[27,512]{1,0:T(8,128)(2,1)S(1)}, u32[]{:S(2)}, u32[]{:S(2)}) collective-permute-start(bf16[27,512]{1,0:T(8,128)(2,1)S(1)} %get-tuple-element.9), channel_id=1, source_target_pairs={{1,0},{2,1},{3,2},{4,3},{5,4},{6,5},{7,6},{8,7},{9,8},{10,9},{11,1... | collective-permute-start | bytes 82952 | tf_op jit(solution)/shard_map/ppermute | solution.py:25
  58.7 3.7 %collective-permute-done.6 = bf16[27,512]{1,0:T(8,128)(2,1)S(1)} collective-permute-done((bf16[27,512]{1,0:T(8,128)(2,1)S(1)}, bf16[27,512]{1,0:T(8,128)(2,1)S(1)}, u32[]{:S(2)}, u32[]{:S(2)}) %collective-permute-start.6) | collective-permute-done | bytes 27680 | tf_op jit(solution)/shard_map/ppermute | solution.py:25
  62.4 3.2 %fusion.9 = bf16[438,512]{1,0:T(8,128)(2,1)S(1)} fusion(bf16[27,512]{1,0:T(8,128)(2,1)S(1)} %collective-permute-done.6, bf16[384,512]{1,0:T(8,128)(2,1)S(1)} %fusion.4, bf16[27,512]{1,0:T(8,128)(2,1)S(1)} %collective-permute-done.5, f32[512]{0:T(512)S(1)} %bitcast.47, f32[512]{0:T(512)S(1)} %bitcast.46), kind=kLoop, calls=%fused_computation.21 | loop fusion | flops 2466816 | bytes 901120 | tf_op jit(solution)/shard_map/convert_element_type | solution.py:38
  65.7 0.1 slice_dynamic-update-slice_fusion.5
  65.8 0.1 slice_dynamic-update-slice_fusion.4
  65.9 0.1 slice_dynamic-update-slice_fusion.3
  66.0 0.1 slice_dynamic-update-slice_fusion.2
  66.1 0.1 slice_dynamic-update-slice_fusion.1
  66.2 0.1 slice_dynamic-update-slice_fusion
  66.3 7.2 %fusion.3 = bf16[384,512]{1,0:T(8,128)(2,1)} fusion(bf16[384,3584]{1,0:T(8,128)(2,1)S(1)} %slice_dynamic-update-slice_fusion, bf16[3584,512]{1,0:T(8,128)(2,1)} %bitcast.43, bf16[384,512]{1,0:T(8,128)(2,1)S(1)} %fusion.4, bf16[3,512,512]{2,1,0:T(8,128)(2,1)} %param.12, f32[512]{0:T(512)S(1)} %bitcast.53, f32[512]{0:T(512)S(1)} %bitcast.55, ...), kind=kOutput, calls=%fused_computation.9 | convolution fusion | flops 1612578816 | bytes 7741440 | tf_op jit(solution)/shard_map/dot_general | solution.py:45
  (24 shorter events, 0.2 us)
Async XLA Ops:
  0.7 17.2 %collective-permute-start = (bf16[8,512]{1,0:T(8,128)(2,1)S(1)}, bf16[8,512]{1,0:T(8,128)(2,1)S(1)}, u32[]{:S(2)}, u32[]{:S(2)}) collective-permute-start(bf16[8,512]{1,0:T(8,128)(2,1)S(1)} %slice_bitcast_fusion.1), channel_id=1, source_target_pairs={{0,1},{1,2},{2,3},{3,4},{4,5},{5,6},{6,7},{7,8},{8,9},{9,10},{10,1... | collective-permute-start | bytes 24584 | tf_op jit(solution)/shard_map/ppermute | solution.py:14
  9.9 7.4 %copy-start.1 = (f32[3,512]{1,0:T(4,128)S(1)}, f32[3,512]{1,0:T(4,128)}, u32[]{:S(2)}) copy-start(f32[3,512]{1,0:T(4,128)} %param.16) | copy-start | bytes 18436
  9.9 8.0 %copy-start = (bf16[2,384,512]{2,1,0:T(8,128)(2,1)S(1)}, bf16[2,384,512]{2,1,0:T(8,128)(2,1)}, u32[]{:S(2)}) copy-start(bf16[2,384,512]{2,1,0:T(8,128)(2,1)} %param.9) | copy-start | bytes 2359300
  9.9 12.5 %copy-start.2 = (f32[3,512]{1,0:T(4,128)S(1)}, f32[3,512]{1,0:T(4,128)}, u32[]{:S(2)}) copy-start(f32[3,512]{1,0:T(4,128)} %param.17) | copy-start | bytes 18436
  18.0 5.0 %collective-permute-start.1 = (bf16[3,512]{1,0:T(4,128)(2,1)S(1)}, bf16[3,512]{1,0:T(4,128)(2,1)S(1)}, u32[]{:S(2)}, u32[]{:S(2)}) collective-permute-start(bf16[3,512]{1,0:T(4,128)(2,1)S(1)} %get-tuple-element.12), channel_id=1, source_target_pairs={{0,1},{1,2},{2,3},{3,4},{4,5},{5,6},{6,7},{7,8},{8,9},{9,10},{10,1... | collective-permute-start | bytes 9224 | tf_op jit(solution)/shard_map/ppermute | solution.py:22
  20.0 5.8 %collective-permute-start.2 = (bf16[3,512]{1,0:T(4,128)(2,1)S(1)}, bf16[3,512]{1,0:T(4,128)(2,1)S(1)}, u32[]{:S(2)}, u32[]{:S(2)}) collective-permute-start(bf16[3,512]{1,0:T(4,128)(2,1)S(1)} %get-tuple-element.13), channel_id=1, source_target_pairs={{1,0},{2,1},{3,2},{4,3},{5,4},{6,5},{7,6},{8,7},{9,8},{10,9},{11,1... | collective-permute-start | bytes 9224 | tf_op jit(solution)/shard_map/ppermute | solution.py:25
  35.8 4.5 %collective-permute-start.3 = (bf16[9,512]{1,0:T(8,128)(2,1)S(1)}, bf16[9,512]{1,0:T(8,128)(2,1)S(1)}, u32[]{:S(2)}, u32[]{:S(2)}) collective-permute-start(bf16[9,512]{1,0:T(8,128)(2,1)S(1)} %get-tuple-element.10), channel_id=1, source_target_pairs={{0,1},{1,2},{2,3},{3,4},{4,5},{5,6},{6,7},{7,8},{8,9},{9,10},{10,1... | collective-permute-start | bytes 27656 | tf_op jit(solution)/shard_map/ppermute | solution.py:22
  37.7 6.0 %collective-permute-start.4 = (bf16[9,512]{1,0:T(8,128)(2,1)S(1)}, bf16[9,512]{1,0:T(8,128)(2,1)S(1)}, u32[]{:S(2)}, u32[]{:S(2)}) collective-permute-start(bf16[9,512]{1,0:T(8,128)(2,1)S(1)} %get-tuple-element.11), channel_id=1, source_target_pairs={{1,0},{2,1},{3,2},{4,3},{5,4},{6,5},{7,6},{8,7},{9,8},{10,9},{11,1... | collective-permute-start | bytes 27656 | tf_op jit(solution)/shard_map/ppermute | solution.py:25
  47.1 0.7 copy-start.7
  47.1 0.7 copy-start.8
  54.3 4.3 %collective-permute-start.5 = (bf16[27,512]{1,0:T(8,128)(2,1)S(1)}, bf16[27,512]{1,0:T(8,128)(2,1)S(1)}, u32[]{:S(2)}, u32[]{:S(2)}) collective-permute-start(bf16[27,512]{1,0:T(8,128)(2,1)S(1)} %get-tuple-element.8), channel_id=1, source_target_pairs={{0,1},{1,2},{2,3},{3,4},{4,5},{5,6},{6,7},{7,8},{8,9},{9,10},{10,1... | collective-permute-start | bytes 82952 | tf_op jit(solution)/shard_map/ppermute | solution.py:22
  56.3 6.1 %collective-permute-start.6 = (bf16[27,512]{1,0:T(8,128)(2,1)S(1)}, bf16[27,512]{1,0:T(8,128)(2,1)S(1)}, u32[]{:S(2)}, u32[]{:S(2)}) collective-permute-start(bf16[27,512]{1,0:T(8,128)(2,1)S(1)} %get-tuple-element.9), channel_id=1, source_target_pairs={{1,0},{2,1},{3,2},{4,3},{5,4},{6,5},{7,6},{8,7},{9,8},{10,9},{11,1... | collective-permute-start | bytes 82952 | tf_op jit(solution)/shard_map/ppermute | solution.py:25
  65.6 0.7 copy-start.3
  65.6 0.7 copy-start.4
  65.6 0.7 copy-start.5
  65.6 0.7 copy-start.6
where the time goes:
time: 74.1 us; the launch traced here: 73.5 us
  matrix products  20.1 us (27%)
  starting transfers between devices  16.9 us (23%)
  local copies, waits for them, and re-layouts  16.7 us (23%)
  waiting for transfers between devices  9.91 us (13%)
  other arithmetic  9.56 us (13%)
    dot_general x3, matrix products, residual_unit(): jnp.dot(gated, pointwise, preferred_element_type=jnp.float32) + bias_point  20.1 us
    ppermute x3, waiting for transfers between devices, with_halo(): lax.ppermute(lax.slice_in_dim(block, 0, width, axis=dim), axis, backward)  9.9 us
    convert_element_type x3, other arithmetic, residual_unit(): snake(inputs.astype(jnp.float32), alpha_in, beta_in).astype(jnp.bfloat16)  9.45 us
    slice x1, local copies, waits for them, and re-layouts, per_device(): taps[index]  7.41 us
    ppermute x3, starting transfers between devices, with_halo(): lax.ppermute(lax.slice_in_dim(block, 0, width, axis=dim), axis, backward)  7.36 us
    ppermute x3, starting transfers between devices, with_halo(): lax.ppermute(lax.slice_in_dim(block, block.shape[dim] - width, None, axis...  5.8 us
    ppermute x1, starting transfers between devices, passed_along(): lax.ppermute(value, axis, [(source, source + steps) for source in range(f...  3.7 us
    unnamed x36, local copies, waits for them, and re-layouts  1.59 us
  transfers between devices with their start and end apart: 7, of which 3 were waited for; matrix products, arithmetic and copies ran while one was open for 19% of the time, Pallas kernels for 0%

commit v1 on v0

v1 whole, which is shorter than its diff:
```python
import functools
import math

import jax
import jax.numpy as jnp
from jax import lax
from jax.experimental import pallas as pl
from jax.experimental.pallas import tpu as pltpu
from jax.sharding import PartitionSpec as P

KERNEL = 7
STRIDE = 8
UNITS = 3
DILATIONS = (1, 3, 9)
SPREAD = 3 * max(DILATIONS)
REACH = 3 * sum(DILATIONS)
ROWS = 16
EDGE = 48
LEAD = EDGE - STRIDE
SINE = (3.141592640130706, -5.167710083507895, 2.550077523214613, -0.5982912856202587, 0.07765766030474007)


def snake(values, frequency, inverse):
    turns = values * frequency
    rest = turns - jnp.round(turns)
    square = rest * rest
    poly = SINE[-1]
    for coefficient in SINE[-2::-1]:
        poly = poly * square + coefficient
    sine = poly * rest
    return values + sine * sine * inverse


def kernel(
    count, frames, tiles, chunks,
    up_ref, low_ref, high_ref, taps_hbm, point_hbm, bias_wide, bias_point,
    alpha_in, beta_in, alpha_mid, beta_mid,
    out_ref,
    taps_ref, point_ref, ext_ref, x_ref, s_ref, sems,
):
    rows = tiles * ROWS
    extended = frames + 2 * EDGE
    copies = []
    for unit in range(UNITS):
        copies.append((
            pltpu.make_async_copy(taps_hbm.at[unit], taps_ref.at[unit], sems.at[0, unit]),
            pltpu.make_async_copy(point_hbm.at[unit], point_ref.at[unit], sems.at[1, unit]),
        ))
    for pair in copies:
        for copy in pair:
            copy.start()
    me = lax.axis_index("tm")
    for part in range(2):
        base = part * extended
        ext_ref[base : base + EDGE, :] = low_ref[part]
        ext_ref[base + EDGE : base + EDGE + frames, :] = up_ref[part]
        ext_ref[base + EDGE + frames : base + extended, :] = high_ref[part]

    def frame_of(row):
        return (row & (ROWS - 1)) * tiles + (row >> 4)

    row = lax.broadcasted_iota(jnp.int32, (rows, 2 * extended), 0)
    column = lax.broadcasted_iota(jnp.int32, (rows, 2 * extended), 1)
    source = frame_of(row)
    hit = (column == source + STRIDE) | (column == source + extended)
    spread = jnp.where(hit, 1.0, 0.0).astype(jnp.bfloat16)
    x_ref[...] = jnp.dot(spread, ext_ref[...], preferred_element_type=jnp.float32).astype(jnp.bfloat16)

    lane_row = lax.broadcasted_iota(jnp.int32, (ROWS, 128), 0) * tiles
    first = LEAD - me * frames
    last = first + count * frames
    channels = x_ref.shape[1]

    for unit in range(UNITS):
        reach = 3 * DILATIONS[unit]
        frequency = alpha_in[unit : unit + 1, :] * (1.0 / math.pi)
        inverse = 1.0 / beta_in[unit : unit + 1, :]
        for tile in range(tiles):
            v = x_ref[tile * ROWS : (tile + 1) * ROWS, :].astype(jnp.float32)
            s = snake(v, frequency, inverse)
            where = lane_row + tile
            inside = (where >= first) & (where < last)
            s = jnp.concatenate(
                [jnp.where(inside, s[:, c : c + 128], 0.0) for c in range(0, channels, 128)], axis=1
            )
            start = (SPREAD + tile) * ROWS
            s_ref[start : start + ROWS, :] = s.astype(jnp.bfloat16)
            if tile >= tiles - reach:
                start = (SPREAD + tile - tiles) * ROWS
                s_ref[start : start + ROWS, :] = pltpu.roll(s, 1, 0).astype(jnp.bfloat16)
            if tile < reach:
                start = (SPREAD + tile + tiles) * ROWS
                s_ref[start : start + ROWS, :] = pltpu.roll(s, ROWS - 1, 0).astype(jnp.bfloat16)
        frequency = alpha_mid[unit : unit + 1, :] * (1.0 / math.pi)
        inverse = 1.0 / beta_mid[unit : unit + 1, :]
        copies[unit][0].wait()
        copies[unit][1].wait()
        begin = 0
        for size in chunks:
            length = size * ROWS
            stacked = jnp.concatenate(
                [
                    s_ref[pl.ds((SPREAD + begin + (k - 3) * DILATIONS[unit]) * ROWS, length), :]
                    for k in range(KERNEL)
                ],
                axis=1,
            )
            h = jnp.dot(stacked, taps_ref[unit], preferred_element_type=jnp.float32)
            h = h + bias_wide[unit : unit + 1, :]
            g = snake(h, frequency, inverse).astype(jnp.bfloat16)
            update = jnp.dot(g, point_ref[unit], preferred_element_type=jnp.float32)
            span = slice(begin * ROWS, begin * ROWS + length)
            kept = x_ref[span, :].astype(jnp.float32)
            x_ref[span, :] = (kept + (update + bias_point[unit : unit + 1, :])).astype(jnp.bfloat16)
            begin += size

    row = lax.broadcasted_iota(jnp.int32, (frames, rows), 0)
    column = lax.broadcasted_iota(jnp.int32, (frames, rows), 1)
    gather = jnp.where(frame_of(column) == row + LEAD, 1.0, 0.0).astype(jnp.bfloat16)
    out_ref[...] = jnp.dot(gather, x_ref[...], preferred_element_type=jnp.float32).astype(jnp.bfloat16)


def per_device(
    upsampled, taps, bias_wide, pointwise, bias_point, alpha_in, beta_in, alpha_mid, beta_mid
):
    count = lax.axis_size("tm")
    frames, channels = upsampled.shape[1:]
    tiles = -(-(frames + LEAD + REACH) // ROWS)
    rows = tiles * ROWS
    forward = [(i, i + 1) for i in range(count - 1)]
    backward = [(i + 1, i) for i in range(count - 1)]
    low = lax.ppermute(upsampled[:, frames - EDGE :], "tm", forward)
    high = lax.ppermute(upsampled[:, :EDGE], "tm", backward)
    half = (tiles + 1) // 2
    vmem = pl.BlockSpec(memory_space=pltpu.VMEM)
    hbm = pl.BlockSpec(memory_space=pl.ANY)
    return pl.pallas_call(
        functools.partial(kernel, count, frames, tiles, (half, tiles - half)),
        out_shape=jax.ShapeDtypeStruct((frames, channels), jnp.bfloat16),
        in_specs=[vmem, vmem, vmem, hbm, hbm] + [vmem] * 6,
        out_specs=vmem,
        scratch_shapes=[
            pltpu.VMEM((UNITS, KERNEL * channels, channels), jnp.bfloat16),
            pltpu.VMEM((UNITS, channels, channels), jnp.bfloat16),
            pltpu.VMEM((2 * (frames + 2 * EDGE), channels), jnp.bfloat16),
            pltpu.VMEM((rows, channels), jnp.bfloat16),
            pltpu.VMEM((rows + 2 * SPREAD * ROWS, channels), jnp.bfloat16),
            pltpu.SemaphoreType.DMA((2, UNITS)),
        ],
        compiler_params=pltpu.CompilerParams(vmem_limit_bytes=48 << 20),
    )(
        upsampled, low, high, taps.reshape(UNITS, KERNEL * channels, channels), pointwise,
        bias_wide, bias_point, alpha_in, beta_in, alpha_mid, beta_mid,
    )


def solution(mesh):
    placed = (P(None, ("grp", "tm"), None), P(), P(), P(), P(), P(), P(), P(), P())
    return jax.shard_map(
        per_device, mesh=mesh, in_specs=placed, out_specs=P(("grp", "tm"), None), check_vma=False
    )
```

time: 74.1 us -> 30.3 us (0.41)
  the two profiles are of different devices: /device:TPU:5 before, /device:TPU:24 now
where the time goes in v1:
time: 30.3 us; the launch traced here: 29.7 us
  Pallas kernels  12.4 us (41%)
  local copies, waits for them, and re-layouts  7.67 us (25%)
  waiting for transfers between devices  4.91 us (16%)
  starting transfers between devices  4.67 us (15%)
    pallas_call x1, Pallas kernels, per_device(): pl.pallas_call(functools.partial(kernel, count, frames, tiles, (half, til...  12.4 us
    unnamed x16, local copies, waits for them, and re-layouts  6.72 us
    ppermute x1, waiting for transfers between devices, per_device(): low = lax.ppermute(upsampled[:, frames - EDGE:], 'tm', forward)  4.64 us
    ppermute x1, starting transfers between devices, per_device(): high = lax.ppermute(upsampled[:, :EDGE], 'tm', backward)  2.75 us
    ppermute x1, starting transfers between devices, per_device(): low = lax.ppermute(upsampled[:, frames - EDGE:], 'tm', forward)  1.92 us
    slice x1, local copies, waits for them, and re-layouts, per_device(): high = lax.ppermute(upsampled[:, :EDGE], 'tm', backward)  0.95 us
  transfers between devices with their start and end apart: 2, of which 2 were waited for; matrix products, arithmetic and copies ran while one was open for 0% of the time, Pallas kernels for 0%

profile of v1, /device:TPU:24, one launch (start us, length us, event | category | flops | bytes accessed | tf_op | source)
XLA Modules:
  0.0 29.7 jit_solution(12256004435659549282)
XLA Ops:
  0.0 1.0 %fusion = (bf16[2,48,512]{2,1,0:T(8,128)(2,1)S(1)}, bf16[2,48,512]{2,1,0:T(8,128)(2,1)S(1)}) fusion(bf16[2,384,512]{2,1,0:T(8,128)(2,1)} %up_ref.1), kind=kLoop, calls=%fused_computation | loop fusion | bytes 393216 | tf_op jit(solution)/shard_map/slice | solution.py:133
  1.0 2.8 %collective-permute-start.1 = (bf16[2,48,512]{2,1,0:T(8,128)(2,1)S(1)}, bf16[2,48,512]{2,1,0:T(8,128)(2,1)S(1)}, u32[]{:S(2)}, u32[]{:S(2)}) collective-permute-start(bf16[2,48,512]{2,1,0:T(8,128)(2,1)S(1)} %get-tuple-element.5), channel_id=1, source_target_pairs={{1,0},{2,1},{3,2},{4,3},{5,4},{6,5},{7,6},{8,7},{9,8},{10,9},{11,1... | collective-permute-start | bytes 294920 | tf_op jit(solution)/shard_map/ppermute | solution.py:133
  3.7 1.9 %collective-permute-start = (bf16[2,48,512]{2,1,0:T(8,128)(2,1)S(1)}, bf16[2,48,512]{2,1,0:T(8,128)(2,1)S(1)}, u32[]{:S(2)}, u32[]{:S(2)}) collective-permute-start(bf16[2,48,512]{2,1,0:T(8,128)(2,1)S(1)} %get-tuple-element.6), channel_id=1, source_target_pairs={{0,1},{1,2},{2,3},{3,4},{4,5},{5,6},{6,7},{7,8},{8,9},{9,10},{10,1... | collective-permute-start | bytes 294920 | tf_op jit(solution)/shard_map/ppermute | solution.py:132
  5.6 0.3 collective-permute-done.1.high_ref
  5.9 4.6 %collective-permute-done.low_ref = bf16[2,48,512]{2,1,0:T(8,128)(2,1)S(1)} collective-permute-done((bf16[2,48,512]{2,1,0:T(8,128)(2,1)S(1)}, bf16[2,48,512]{2,1,0:T(8,128)(2,1)S(1)}, u32[]{:S(2)}, u32[]{:S(2)}) %collective-permute-start) | collective-permute-done | bytes 98336 | tf_op jit(solution)/shard_map/ppermute | solution.py:132
  10.6 0.0 copy-start
  10.6 1.4 %copy-done = bf16[3,512,512]{2,1,0:T(8,128)(2,1)S(1)} copy-done((bf16[3,512,512]{2,1,0:T(8,128)(2,1)S(1)}, bf16[3,512,512]{2,1,0:T(8,128)(2,1)}, u32[]{:S(2)}) %copy-start) | copy-done | bytes 1572888
  12.0 0.0 copy-start.1
  12.0 1.1 %copy-done.1 = bf16[2,384,512]{2,1,0:T(8,128)(2,1)S(1)} copy-done((bf16[2,384,512]{2,1,0:T(8,128)(2,1)S(1)}, bf16[2,384,512]{2,1,0:T(8,128)(2,1)}, u32[]{:S(2)}) %copy-start.1) | copy-done | bytes 786456
  13.1 0.0 copy-start.2
  13.1 0.7 %copy-done.2 = f32[3,512]{1,0:T(4,128)S(1)} copy-done((f32[3,512]{1,0:T(4,128)S(1)}, f32[3,512]{1,0:T(4,128)}, u32[]{:S(2)}) %copy-start.2) | copy-done | bytes 6168
  13.8 0.0 copy-start.3
  13.8 0.7 %copy-done.3 = f32[3,512]{1,0:T(4,128)S(1)} copy-done((f32[3,512]{1,0:T(4,128)S(1)}, f32[3,512]{1,0:T(4,128)}, u32[]{:S(2)}) %copy-start.3) | copy-done | bytes 6168
  14.5 0.0 copy-start.4
  14.5 0.7 %copy-done.4 = f32[3,512]{1,0:T(4,128)S(1)} copy-done((f32[3,512]{1,0:T(4,128)S(1)}, f32[3,512]{1,0:T(4,128)}, u32[]{:S(2)}) %copy-start.4) | copy-done | bytes 6168
  15.2 0.0 copy-start.5
  15.2 0.7 %copy-done.5 = f32[3,512]{1,0:T(4,128)S(1)} copy-done((f32[3,512]{1,0:T(4,128)S(1)}, f32[3,512]{1,0:T(4,128)}, u32[]{:S(2)}) %copy-start.5) | copy-done | bytes 6168
  15.9 0.0 copy-start.6
  15.9 0.7 %copy-done.6 = f32[3,512]{1,0:T(4,128)S(1)} copy-done((f32[3,512]{1,0:T(4,128)S(1)}, f32[3,512]{1,0:T(4,128)}, u32[]{:S(2)}) %copy-start.6) | copy-done | bytes 6168
  16.6 0.0 copy-start.7
  16.6 0.7 %copy-done.7 = f32[3,512]{1,0:T(4,128)S(1)} copy-done((f32[3,512]{1,0:T(4,128)S(1)}, f32[3,512]{1,0:T(4,128)}, u32[]{:S(2)}) %copy-start.7) | copy-done | bytes 6168
  17.3 12.4 %shard_map.91 = bf16[384,512]{1,0:T(8,128)(2,1)} custom-call(bf16[2,384,512]{2,1,0:T(8,128)(2,1)S(1)} %copy-done.1, bf16[2,48,512]{2,1,0:T(8,128)(2,1)S(1)} %collective-permute-done.low_ref, bf16[2,48,512]{2,1,0:T(8,128)(2,1)S(1)} %collective-permute-done.1.high_ref, bf16[3,3584,512]{2,1,0:T(8,128)(2,1)} %bitcast.1, bf16[3,512,512]{2,1,0:T(8,128)(2,1)S(1)} %copy-done, ...), custom_call_target="tpu_custom_call" | custom-call | tf_op jit(solution)/shard_map/pallas_call | solution.py:137
Async XLA Ops:
  1.0 5.0 %collective-permute-start.1 = (bf16[2,48,512]{2,1,0:T(8,128)(2,1)S(1)}, bf16[2,48,512]{2,1,0:T(8,128)(2,1)S(1)}, u32[]{:S(2)}, u32[]{:S(2)}) collective-permute-start(bf16[2,48,512]{2,1,0:T(8,128)(2,1)S(1)} %get-tuple-element.5), channel_id=1, source_target_pairs={{1,0},{2,1},{3,2},{4,3},{5,4},{6,5},{7,6},{8,7},{9,8},{10,9},{11,1... | collective-permute-start | bytes 294920 | tf_op jit(solution)/shard_map/ppermute | solution.py:133
  3.7 6.8 %collective-permute-start = (bf16[2,48,512]{2,1,0:T(8,128)(2,1)S(1)}, bf16[2,48,512]{2,1,0:T(8,128)(2,1)S(1)}, u32[]{:S(2)}, u32[]{:S(2)}) collective-permute-start(bf16[2,48,512]{2,1,0:T(8,128)(2,1)S(1)} %get-tuple-element.6), channel_id=1, source_target_pairs={{0,1},{1,2},{2,3},{3,4},{4,5},{5,6},{6,7},{7,8},{8,9},{9,10},{10,1... | collective-permute-start | bytes 294920 | tf_op jit(solution)/shard_map/ppermute | solution.py:132
  10.6 1.4 %copy-start = (bf16[3,512,512]{2,1,0:T(8,128)(2,1)S(1)}, bf16[3,512,512]{2,1,0:T(8,128)(2,1)}, u32[]{:S(2)}) copy-start(bf16[3,512,512]{2,1,0:T(8,128)(2,1)} %point_hbm.1) | copy-start | bytes 4718596
  12.0 1.1 %copy-start.1 = (bf16[2,384,512]{2,1,0:T(8,128)(2,1)S(1)}, bf16[2,384,512]{2,1,0:T(8,128)(2,1)}, u32[]{:S(2)}) copy-start(bf16[2,384,512]{2,1,0:T(8,128)(2,1)} %up_ref.1) | copy-start | bytes 2359300
  13.1 0.7 %copy-start.2 = (f32[3,512]{1,0:T(4,128)S(1)}, f32[3,512]{1,0:T(4,128)}, u32[]{:S(2)}) copy-start(f32[3,512]{1,0:T(4,128)} %bias_wide.1) | copy-start | bytes 18436
  13.8 0.7 %copy-start.3 = (f32[3,512]{1,0:T(4,128)S(1)}, f32[3,512]{1,0:T(4,128)}, u32[]{:S(2)}) copy-start(f32[3,512]{1,0:T(4,128)} %bias_point.1) | copy-start | bytes 18436
  14.5 0.7 %copy-start.4 = (f32[3,512]{1,0:T(4,128)S(1)}, f32[3,512]{1,0:T(4,128)}, u32[]{:S(2)}) copy-start(f32[3,512]{1,0:T(4,128)} %alpha_in.1) | copy-start | bytes 18436
  15.2 0.7 %copy-start.5 = (f32[3,512]{1,0:T(4,128)S(1)}, f32[3,512]{1,0:T(4,128)}, u32[]{:S(2)}) copy-start(f32[3,512]{1,0:T(4,128)} %beta_in.1) | copy-start | bytes 18436
  15.9 0.7 %copy-start.6 = (f32[3,512]{1,0:T(4,128)S(1)}, f32[3,512]{1,0:T(4,128)}, u32[]{:S(2)}) copy-start(f32[3,512]{1,0:T(4,128)} %alpha_mid.1) | copy-start | bytes 18436
  16.6 0.7 %copy-start.7 = (f32[3,512]{1,0:T(4,128)S(1)}, f32[3,512]{1,0:T(4,128)}, u32[]{:S(2)}) copy-start(f32[3,512]{1,0:T(4,128)} %beta_mid.1) | copy-start | bytes 18436

commit v2 on v1

--- a/solution.py
+++ b/solution.py
@@ -8,6 +8,7 @@
 from jax.experimental.pallas import tpu as pltpu
 from jax.sharding import PartitionSpec as P
 
+MESH = pl.DeviceIdType.MESH
 KERNEL = 7
 STRIDE = 8
 UNITS = 3
@@ -33,28 +34,89 @@
 
 def kernel(
     count, frames, tiles, chunks,
-    up_ref, low_ref, high_ref, taps_hbm, point_hbm, bias_wide, bias_point,
-    alpha_in, beta_in, alpha_mid, beta_mid,
+    up_hbm, taps_hbm, bias_wide_hbm, point_hbm, bias_point_hbm,
+    alpha_in_hbm, beta_in_hbm, alpha_mid_hbm, beta_mid_hbm,
     out_ref,
-    taps_ref, point_ref, ext_ref, x_ref, s_ref, sems,
+    taps_ref, point_ref, ext_ref, x_ref, s_ref,
+    bias_wide, bias_point, alpha_in, beta_in, alpha_mid, beta_mid,
+    taps_sems, point_sems, small_sems, up_sem, send_sems, recv_sems,
 ):
     rows = tiles * ROWS
     extended = frames + 2 * EDGE
-    copies = []
-    for unit in range(UNITS):
-        copies.append((
-            pltpu.make_async_copy(taps_hbm.at[unit], taps_ref.at[unit], sems.at[0, unit]),
-            pltpu.make_async_copy(point_hbm.at[unit], point_ref.at[unit], sems.at[1, unit]),
+    me = lax.axis_index("tm")
+    has_left = me > 0
+    has_right = me < count - 1
+    barrier = pltpu.get_barrier_semaphore()
+
+    @pl.when(has_left)
+    def _():
+        pl.semaphore_signal(barrier, inc=1, device_id={"tm": me - 1}, device_id_type=MESH)
+
+    @pl.when(has_right)
+    def _():
+        pl.semaphore_signal(barrier, inc=1, device_id={"tm": me + 1}, device_id_type=MESH)
+
+    own = pltpu.make_async_copy(up_hbm, ext_ref.at[:, pl.ds(EDGE, frames), :], up_sem)
+    own.start()
+    smalls = [
+        pltpu.make_async_copy(source, target, small_sems.at[i])
+        for i, (source, target) in enumerate((
+            (alpha_in_hbm, alpha_in), (beta_in_hbm, beta_in), (bias_wide_hbm, bias_wide),
+            (alpha_mid_hbm, alpha_mid), (beta_mid_hbm, beta_mid), (bias_point_hbm, bias_point),
         ))
+    ]
+    for copy in smalls:
+        copy.start()
+    copies = [
+        (
+            pltpu.make_async_copy(taps_hbm.at[unit], taps_ref.at[unit], taps_sems.at[unit]),
+            pltpu.make_async_copy(point_hbm.at[unit], point_ref.at[unit], point_sems.at[unit]),
+        )
+        for unit in range(UNITS)
+    ]
+    copies[0][0].start()
+
+    @pl.when(has_left & has_right)
+    def _():
+        pl.semaphore_wait(barrier, 2)
+
+    @pl.when(has_left != has_right)
+    def _():
+        pl.semaphore_wait(barrier, 1)
+
+    to_right = pltpu.make_async_remote_copy(
+        src_ref=up_hbm.at[:, pl.ds(frames - EDGE, EDGE), :],
+        dst_ref=ext_ref.at[:, pl.ds(0, EDGE), :],
+        send_sem=send_sems.at[0], recv_sem=recv_sems.at[0],
+        device_id={"tm": me + 1}, device_id_type=MESH,
+    )
+    to_left = pltpu.make_async_remote_copy(
+        src_ref=up_hbm.at[:, pl.ds(0, EDGE), :],
+        dst_ref=ext_ref.at[:, pl.ds(EDGE + frames, EDGE), :],
+        send_sem=send_sems.at[1], recv_sem=recv_sems.at[1],
+        device_id={"tm": me - 1}, device_id_type=MESH,
+    )
+
+    @pl.when(has_right)
+    def _():
+        to_right.start()
+
+    @pl.when(has_left)
+    def _():
+        to_left.start()
+
     for pair in copies:
         for copy in pair:
-            copy.start()
-    me = lax.axis_index("tm")
-    for part in range(2):
-        base = part * extended
-        ext_ref[base : base + EDGE, :] = low_ref[part]
-        ext_ref[base + EDGE : base + EDGE + frames, :] = up_ref[part]
-        ext_ref[base + EDGE + frames : base + extended, :] = high_ref[part]
+            if copy is not copies[0][0]:
+                copy.start()
+
+    @pl.when(jnp.logical_not(has_left))
+    def _():
+        ext_ref[:, 0:EDGE, :] = jnp.zeros((2, EDGE, ext_ref.shape[2]), jnp.bfloat16)
+
+    @pl.when(jnp.logical_not(has_right))
+    def _():
+        ext_ref[:, EDGE + frames : extended, :] = jnp.zeros((2, EDGE, ext_ref.shape[2]), jnp.bfloat16)
 
     def frame_of(row):
         return (row & (ROWS - 1)) * tiles + (row >> 4)
@@ -64,7 +126,20 @@
     source = frame_of(row)
     hit = (column == source + STRIDE) | (column == source + extended)
     spread = jnp.where(hit, 1.0, 0.0).astype(jnp.bfloat16)
-    x_ref[...] = jnp.dot(spread, ext_ref[...], preferred_element_type=jnp.float32).astype(jnp.bfloat16)
+    for copy in smalls:
+        copy.wait()
+    own.wait()
+
+    @pl.when(has_left)
+    def _():
+        to_right.wait_recv()
+
+    @pl.when(has_right)
+    def _():
+        to_left.wait_recv()
+
+    both = ext_ref[...].reshape(2 * extended, ext_ref.shape[2])
+    x_ref[...] = jnp.dot(spread, both, preferred_element_type=jnp.float32).astype(jnp.bfloat16)
 
     lane_row = lax.broadcasted_iota(jnp.int32, (ROWS, 128), 0) * tiles
     first = LEAD - me * frames
@@ -114,6 +189,14 @@
             x_ref[span, :] = (kept + (update + bias_point[unit : unit + 1, :])).astype(jnp.bfloat16)
             begin += size
 
+    @pl.when(has_right)
+    def _():
+        to_right.wait_send()
+
+    @pl.when(has_left)
+    def _():
+        to_left.wait_send()
+
     row = lax.broadcasted_iota(jnp.int32, (frames, rows), 0)
     column = lax.broadcasted_iota(jnp.int32, (frames, rows), 1)
     gather = jnp.where(frame_of(column) == row + LEAD, 1.0, 0.0).astype(jnp.bfloat16)
@@ -127,30 +210,36 @@
     frames, channels = upsampled.shape[1:]
     tiles = -(-(frames + LEAD + REACH) // ROWS)
     rows = tiles * ROWS
-    forward = [(i, i + 1) for i in range(count - 1)]
-    backward = [(i + 1, i) for i in range(count - 1)]
-    low = lax.ppermute(upsampled[:, frames - EDGE :], "tm", forward)
-    high = lax.ppermute(upsampled[:, :EDGE], "tm", backward)
     half = (tiles + 1) // 2
     vmem = pl.BlockSpec(memory_space=pltpu.VMEM)
-    hbm = pl.BlockSpec(memory_space=pl.ANY)
+    hbm = pl.BlockSpec(memory_space=pltpu.HBM)
     return pl.pallas_call(
         functools.partial(kernel, count, frames, tiles, (half, tiles - half)),
         out_shape=jax.ShapeDtypeStruct((frames, channels), jnp.bfloat16),
-        in_specs=[vmem, vmem, vmem, hbm, hbm] + [vmem] * 6,
+        in_specs=[hbm] * 9,
         out_specs=vmem,
         scratch_shapes=[
             pltpu.VMEM((UNITS, KERNEL * channels, channels), jnp.bfloat16),
             pltpu.VMEM((UNITS, channels, channels), jnp.bfloat16),
-            pltpu.VMEM((2 * (frames + 2 * EDGE), channels), jnp.bfloat16),
+            pltpu.VMEM((2, frames + 2 * EDGE, channels), jnp.bfloat16),
             pltpu.VMEM((rows, channels), jnp.bfloat16),
             pltpu.VMEM((rows + 2 * SPREAD * ROWS, channels), jnp.bfloat16),
-            pltpu.SemaphoreType.DMA((2, UNITS)),
+        ]
+        + [pltpu.VMEM((UNITS, channels), jnp.float32)] * 6
+        + [
+            pltpu.SemaphoreType.DMA((UNITS,)),
+            pltpu.SemaphoreType.DMA((UNITS,)),
+            pltpu.SemaphoreType.DMA((6,)),
+            pltpu.SemaphoreType.DMA,
+            pltpu.SemaphoreType.DMA((2,)),
+            pltpu.SemaphoreType.DMA((2,)),
         ],
-        compiler_params=pltpu.CompilerParams(vmem_limit_bytes=48 << 20),
+        compiler_params=pltpu.CompilerParams(
+            vmem_limit_bytes=63 << 20, collective_id=0, has_side_effects=True
+        ),
     )(
-        upsampled, low, high, taps.reshape(UNITS, KERNEL * channels, channels), pointwise,
-        bias_wide, bias_point, alpha_in, beta_in, alpha_mid, beta_mid,
+        upsampled, taps.reshape(UNITS, KERNEL * channels, channels), bias_wide, pointwise,
+        bias_point, alpha_in, beta_in, alpha_mid, beta_mid,
     )
 
 

time: 30.3 us -> 19.3 us (0.64)
  the two profiles are of different devices: /device:TPU:24 before, /device:TPU:25 now
where the time goes in v2:
time: 19.3 us; the launch traced here: 19.1 us
  Pallas kernels  17.4 us (90%)
  local copies, waits for them, and re-layouts  1.77 us (9%)
    pallas_call x1, Pallas kernels, per_device(): pl.pallas_call(functools.partial(kernel, count, frames, tiles, (half, til...  17.4 us
    unnamed x1, local copies, waits for them, and re-layouts  1.77 us

profile of v2, /device:TPU:25, one launch (start us, length us, event | category | flops | bytes accessed | tf_op | source)
XLA Modules:
  0.0 19.1 jit_solution(257117990109331654)
XLA Ops:
  0.0 17.4 %shard_map.91 = bf16[384,512]{1,0:T(8,128)(2,1)} custom-call(bf16[2,384,512]{2,1,0:T(8,128)(2,1)} %up_hbm.1, bf16[3,3584,512]{2,1,0:T(8,128)(2,1)} %bitcast.1, f32[3,512]{1,0:T(4,128)} %bias_wide_hbm.1, bf16[3,512,512]{2,1,0:T(8,128)(2,1)} %point_hbm.1, f32[3,512]{1,0:T(4,128)} %bias_point_hbm.1, f32[3,512]{1,0:T(4,128)} %alpha_in_hbm.1, ...), custom_call_target="tpu_custom_call" | custom-call | tf_op jit(solution)/shard_map/pallas_call | solution.py:216
  17.4 1.8 %copy.11 = bf16[384,512]{1,0:T(8,128)(2,1)} copy(bf16[384,512]{1,0:T(8,128)(2,1)} %shard_map.91) | data formatting | bytes 786432
